TPU v7x, 32 devices: a whole 2x2x4 slice. The times are simulated.
32 devices in a mesh: groups: 2 (over y), tok: 16 (over z, x, core).
Axes of the slice: x: 2, y: 2, z: 4, core: 2. Of those that a mesh axis runs over, the one named last changes fastest.
Arguments:
- queries: bfloat16 [1024, 2048], P(('groups', 'tok')), parts along dimension 0, may hold values from -6 to 6
- new_kv: bfloat16 [3072, 4096], P(('groups', 'tok')), parts along dimension 0, may hold values from -6 to 6
- prev_kv: bfloat16 [2, 3072, 4096], P(None, ('groups', 'tok')), parts along dimension 1, may hold values from -6 to 6
- base_step: int32 [32], P(('groups', 'tok')), parts along dimension 0, may hold values from 0 to 1
- live_counts: int32 [32], P('groups'), parts along dimension 0, may hold values from 1 to 96
- sketch: float32 [4096, 32], replicated, may hold values from -0.09375 to 0.09375
- cache: bfloat16 [64, 1536, 128], P(('groups', 'tok')), parts along dimension 0, may hold values from -6 to 6, as said below
- w_out: bfloat16 [2048, 1536], replicated, may hold values from -0.125 to 0.125
Outputs:
- projected: bfloat16 [1024, 1536], P(('groups', 'tok')), parts along dimension 0
There are 2 independent parts, one for each index of `groups`. A program takes and returns all parts, laid end to end along the dimension named above; an argument that names none is the same for every part. Nothing has to cross between parts.
Inputs may be any that keep to these rules, and one draw needn't show every extreme that they name: cache slots i and j hold the same values when i // 2 == j // 2 and i % 2 == j % 2.
All inputs are finite; a program needn't handle non-finite values.
Results may differ from a plain program's by a relative error of at most 0.019.
Values may be sent and summed in bfloat16 or wider, within the bound.
No kernel may reach another device: no remote copies, remote signals or barrier semaphores. Data moves between devices by JAX's collectives and lax.ppermute only.
A program may use at most 128 MiB of HBM per device.

v0:
```python
import math
import jax
import jax.numpy as jnp
from jax import lax
from jax.sharding import PartitionSpec as P

HD = 64
SWEEPS = 2
highest = lax.Precision.HIGHEST


def orthonormal(block_cols):
    gram_matrix = jnp.dot(block_cols.T, block_cols, precision=highest)
    lower_factor = jnp.linalg.cholesky(gram_matrix)
    return jax.scipy.linalg.solve_triangular(lower_factor, block_cols.T, lower=True).T


def compress(delta_block, sketch):
    basis_cols = orthonormal(jnp.dot(delta_block, sketch, precision=highest))
    for sweep_index in range(SWEEPS):
        inner = jnp.dot(delta_block.T, basis_cols, precision=highest)
        basis_cols = orthonormal(jnp.dot(delta_block, inner, precision=highest))
    right_factor = jnp.dot(basis_cols.T, delta_block, precision=highest)
    return (basis_cols.astype(jnp.bfloat16), right_factor.astype(jnp.bfloat16))


def spread_heads(matrix, head_groups, groups_q, width):
    lead = matrix.shape[0]
    per_group = matrix.reshape(lead, head_groups, width).transpose(1, 0, 2)
    copies = jnp.broadcast_to(per_group[:, None], (head_groups, groups_q, lead, width))
    return copies.reshape(head_groups * groups_q, lead, width)


def attend_head(pieces, live_keys):
    q_head, keys_values = pieces
    key_part = keys_values[:, :HD]
    value_part = keys_values[:, HD:]
    query_count = q_head.shape[0]
    block_rows = math.gcd(query_count, 512)

    def one_block(query_block):
        scores = jnp.dot(query_block, key_part.T, preferred_element_type=jnp.float32) * HD ** (-0.5)
        scores = jnp.where(live_keys[None, :], scores, -1e30)
        row_max = jnp.max(scores, axis=-1, keepdims=True)
        exponent = jnp.exp(scores - row_max)
        weights = (exponent / jnp.sum(exponent, axis=-1, keepdims=True)).astype(jnp.bfloat16)
        return jnp.dot(weights, value_part, preferred_element_type=jnp.float32).astype(jnp.bfloat16)

    return lax.map(one_block, q_head.reshape(query_count // block_rows, block_rows, HD)).reshape(
        query_count, HD
    )


def per_device(queries, new_kv, prev_kv, base_step, live_counts, sketch, cache, w_out):
    shards = lax.axis_size("tok")
    tok_rows = new_kv.shape[0]
    query_rows = queries.shape[0]
    head_count = queries.shape[1] // HD
    groups_q = max(1, shards // head_count)
    per_dev = head_count * groups_q // shards
    head_groups = head_count // per_dev
    part_rows = query_rows // groups_q
    width = per_dev * 2 * HD
    key_count = shards * tok_rows
    query_count = shards * part_rows
    prior = prev_kv[0].astype(jnp.float32)
    prior = jnp.where(base_step[0] == 1, prev_kv[1].astype(jnp.float32), prior)
    delta = new_kv.astype(jnp.float32) - prior
    left_factor, right_factor = compress(delta, sketch)
    rank_cols = left_factor.shape[1]
    q_blocks = queries.reshape(groups_q, part_rows, head_groups, per_dev * HD)
    q_blocks = q_blocks.transpose(2, 0, 1, 3).reshape(shards, part_rows, per_dev * HD)
    w_blocks = spread_heads(right_factor, head_groups, groups_q, width)
    q_here = lax.all_to_all(q_blocks, "tok", split_axis=0, concat_axis=0, tiled=True)
    u_here = lax.all_gather(left_factor, "tok", axis=0, tiled=True).reshape(
        shards, tok_rows, rank_cols
    )
    w_here = lax.all_to_all(w_blocks, "tok", split_axis=0, concat_axis=0, tiled=True)
    lowrank = jnp.einsum("str,src->stc", u_here, w_here, preferred_element_type=jnp.float32).astype(
        jnp.bfloat16
    )
    lowrank = lowrank.reshape(key_count, per_dev, 2 * HD).transpose(1, 0, 2)
    keys_values = (cache.astype(jnp.float32) + lowrank.astype(jnp.float32)).astype(jnp.bfloat16)
    live_keys = (jnp.arange(tok_rows, dtype=jnp.int32)[None, :] < live_counts[:, None]).reshape(
        key_count
    )
    q_heads = q_here.reshape(query_count, per_dev, HD).transpose(1, 0, 2)
    attended = lax.map(lambda pieces: attend_head(pieces, live_keys), (q_heads, keys_values))
    attended = attended.transpose(1, 0, 2).reshape(shards, part_rows, per_dev * HD)
    returned = lax.all_to_all(attended, "tok", split_axis=0, concat_axis=0, tiled=True)
    returned = returned.reshape(head_groups, groups_q, part_rows, per_dev * HD)
    row_block = returned.transpose(1, 2, 0, 3).reshape(query_rows, head_count * HD)
    return jnp.dot(row_block, w_out, preferred_element_type=jnp.float32).astype(jnp.bfloat16)


def solution(mesh):
    return jax.shard_map(
        per_device,
        mesh=mesh,
        in_specs=(
            P(("groups", "tok"), None),
            P(("groups", "tok"), None),
            P(None, ("groups", "tok"), None),
            P(("groups", "tok")),
            P("groups"),
            P(),
            P(("groups", "tok"), None, None),
            P(),
        ),
        out_specs=P(("groups", "tok"), None),
        check_vma=False,
    )
```

profile of v0, /device:TPU:0, one launch (start us, length us, event | category | flops | bytes accessed | tf_op | source)
XLA Modules:
  0.0 94.7 jit_solution(8483638808945009714)
XLA Ops:
  0.0 0.0 copy-start
  0.0 1.0 %copy.33 = bf16[4,8,16,128]{3,2,1,0:T(8,128)(2,1)S(1)} copy(bf16[4,8,16,128]{3,1,2,0:T(8,128)(2,1)} %bitcast.116) | data formatting | bytes 262144
  1.0 0.7 copy.43
  1.7 7.4 %all-to-all-start = ((bf16[16,32,128]{2,1,0:T(8,128)(2,1)}), bf16[16,32,128]{2,1,0:T(8,128)(2,1)S(1)}, u32[]{:S(2)}, u32[]{:S(2)}) async-start(bf16[16,32,128]{2,1,0:T(8,128)(2,1)} %bitcast.103), calls=%async_computation | async-start | bytes 262144 | tf_op jit(solution)/shard_map/all_to_all | solution.py:74
  9.7 1.9 %bitcast_subtract_fusion = f32[96,4096]{1,0:T(8,128)S(1)} fusion(bf16[96,4096]{1,0:T(8,128)(2,1)} %param.14, bf16[2,96,4096]{2,1,0:T(8,128)(2,1)} %param.15, pred[]{:T(512)} %bitcast.3), kind=kLoop, calls=%fused_computation.21 | loop fusion | flops 1966080 | bytes 3932161 | tf_op jit(solution)/shard_map/sub | solution.py:68
  11.6 0.0 copy-done
  11.6 1.3 %fusion.37 = f32[96,32]{0,1:T(8,128)S(1)} fusion(f32[96,4096]{1,0:T(8,128)S(1)} %bitcast_subtract_fusion, f32[4096,32]{0,1:T(8,128)S(1)} %copy-done), kind=kOutput, calls=%fused_computation.61 | convolution fusion | flops 150994944 | bytes 2109440 | tf_op jit(solution)/shard_map/dot_general | solution.py:19
  13.0 0.1 fusion.38
  13.1 0.1 copy.24
  13.2 2.9 %cholesky.59 = f32[32,32]{1,0:T(8,128)S(1)} custom-call(f32[32,32]{1,0:T(8,128)S(1)} %fusion.31), custom_call_target="Cholesky" | custom-call | tf_op jit(solution)/shard_map/jit(cholesky)/cholesky | solution.py:14
  16.2 0.6 compare_reduce_fusion.2
  16.8 0.7 fusion.17
  17.5 2.4 %custom-call.7 = f32[1,32,32]{1,2,0:T(8,128)S(1)} custom-call(f32[1,32,32]{2,1,0:T(8,128)S(1)} %fusion.17), custom_call_target="InvertDiagBlocksLowerTriangular" | custom-call | tf_op jit(solution)/shard_map/jit(_solve_triangular)/triangular_solve | solution.py:15
  19.9 0.2 fusion.28
  20.1 1.0 %fusion.39 = f32[4096,32]{0,1:T(8,128)S(1)} fusion(f32[96,4096]{1,0:T(8,128)S(1)} %bitcast_subtract_fusion, f32[32,96]{1,0:T(8,128)S(1)} %fusion.28), kind=kOutput, calls=%fused_computation.63 | convolution fusion | flops 150994944 | bytes 2109440 | tf_op jit(solution)/shard_map/dot_general | solution.py:21
  21.2 1.3 %fusion.40 = f32[96,32]{0,1:T(8,128)S(1)} fusion(f32[96,4096]{1,0:T(8,128)S(1)} %bitcast_subtract_fusion, f32[4096,32]{0,1:T(8,128)S(1)} %fusion.39), kind=kOutput, calls=%fused_computation.64 | convolution fusion | flops 150994944 | bytes 2109440 | tf_op jit(solution)/shard_map/dot_general | solution.py:22
  22.5 0.1 fusion.41
  22.7 0.1 copy.25
  22.7 2.9 %cholesky.70 = f32[32,32]{1,0:T(8,128)S(1)} custom-call(f32[32,32]{1,0:T(8,128)S(1)} %fusion.27), custom_call_target="Cholesky" | custom-call | tf_op jit(solution)/shard_map/jit(cholesky)/cholesky | solution.py:14
  25.7 0.6 compare_reduce_fusion.1
  26.3 0.7 fusion.18
  27.0 2.4 %custom-call.8 = f32[1,32,32]{1,2,0:T(8,128)S(1)} custom-call(f32[1,32,32]{2,1,0:T(8,128)S(1)} %fusion.18), custom_call_target="InvertDiagBlocksLowerTriangular" | custom-call | tf_op jit(solution)/shard_map/jit(_solve_triangular)/triangular_solve | solution.py:15
  29.4 0.2 fusion.24
  29.7 1.0 %fusion.42 = f32[4096,32]{0,1:T(8,128)S(1)} fusion(f32[96,4096]{1,0:T(8,128)S(1)} %bitcast_subtract_fusion, f32[32,96]{1,0:T(8,128)S(1)} %fusion.24), kind=kOutput, calls=%fused_computation.66 | convolution fusion | flops 150994944 | bytes 2109440 | tf_op jit(solution)/shard_map/dot_general | solution.py:21
  30.7 1.3 %fusion.43 = f32[96,32]{0,1:T(8,128)S(1)} fusion(f32[96,4096]{1,0:T(8,128)S(1)} %bitcast_subtract_fusion, f32[4096,32]{0,1:T(8,128)S(1)} %fusion.42), kind=kOutput, calls=%fused_computation.67 | convolution fusion | flops 150994944 | bytes 2109440 | tf_op jit(solution)/shard_map/dot_general | solution.py:22
  32.0 0.1 fusion.44
  32.2 0.1 copy.26
  32.3 2.9 %cholesky.81 = f32[32,32]{1,0:T(8,128)S(1)} custom-call(f32[32,32]{1,0:T(8,128)S(1)} %fusion.23), custom_call_target="Cholesky" | custom-call | tf_op jit(solution)/shard_map/jit(cholesky)/cholesky | solution.py:14
  35.2 0.6 compare_reduce_fusion
  35.9 0.7 fusion.19
  36.5 2.4 %custom-call.9 = f32[1,32,32]{1,2,0:T(8,128)S(1)} custom-call(f32[1,32,32]{2,1,0:T(8,128)S(1)} %fusion.19), custom_call_target="InvertDiagBlocksLowerTriangular" | custom-call | tf_op jit(solution)/shard_map/jit(_solve_triangular)/triangular_solve | solution.py:15
  39.0 0.2 fusion.20
  39.2 0.9 convolution_convert_fusion
  40.1 0.7 copy.42
  40.8 0.0 all-to-all-done
  40.8 6.0 %all-to-all-start.1 = ((bf16[16,32,256]{2,1,0:T(8,128)(2,1)}), bf16[16,32,256]{2,1,0:T(8,128)(2,1)S(1)}, u32[]{:S(2)}, u32[]{:S(2)}) async-start(bf16[16,32,256]{2,1,0:T(8,128)(2,1)} %bitcast.102), calls=%async_computation.1 | async-start | bytes 524288 | tf_op jit(solution)/shard_map/all_to_all | solution.py:78
  46.8 22.3 %all-gather = bf16[16,96,32]{1,2,0:T(8,128)(2,1)S(1)} all-gather(bf16[1,96,32]{1,2,0:T(8,128)(2,1)S(1)} %convert_bitcast_fusion), channel_id=1, replica_groups=mesh['groups'=2,'tok'=16] {'tok'}, dimensions={0}, use_global_device_ids=true | all-gather | bytes 104448 | tf_op jit(solution)/shard_map/all_gather | solution.py:75
  69.2 0.1 reshape.49
  69.4 0.0 all-to-all-done.1
  69.4 1.6 %fusion.14 = f32[16,96,256]{2,1,0:T(8,128)} fusion(bf16[16,96,32]{1,2,0:T(8,128)(2,1)S(1)} %all-gather, bf16[16,32,256]{2,1,0:T(8,128)(2,1)S(1)} %all-to-all-done.1), kind=kOutput, calls=%fused_computation.23 | convolution fusion | flops 25952256 | bytes 1933312 | tf_op jit(solution)/shard_map/str,src->stc/dot_general | solution.py:79
  71.0 2.1 %reshape.55 = f32[1536,2,128]{2,1,0:T(2,128)S(1)} reshape(f32[16,96,256]{2,1,0:T(8,128)} %fusion.14) | data formatting | bytes 3145728 | tf_op jit(solution)/shard_map/convert_element_type | solution.py:83
  73.0 0.0 copy-start.1
  73.0 1.3 %fusion.13 = bf16[2,1536,128]{2,1,0:T(8,128)(2,1)S(1)} fusion(f32[1536,2,128]{2,1,0:T(2,128)S(1)} %reshape.55, bf16[2,1536,128]{2,1,0:T(8,128)(2,1)} %param.19), kind=kLoop, calls=%fused_computation.20 | loop fusion | flops 1179648 | bytes 3145728 | tf_op jit(solution)/shard_map/convert_element_type | solution.py:83
  74.3 0.0 copy-done.1
  74.3 4.9 %while.11 = (s32[]{:T(128)}, bf16[2,512,64]{1,2,0:T(8,128)(2,1)S(1)}, bf16[2,512,64]{2,1,0:T(8,128)(2,1)S(1)}, bf16[2,1536,128]{2,1,0:T(8,128)(2,1)S(1)}, s32[16]{0:T(128)S(1)}, /*index=5*/s32[]{:T(128)}) while((s32[]{:T(128)}, bf16[2,512,64]{1,2,0:T(8,128)(2,1)S(1)}, bf16[2,512,64]{2,1,0:T(8,128)(2,1)S(1)}, ...), condition=%wide.region_5.8_spmd.clone, body=%wide.region_2.7_spmd.clone.sunk | while | flops 207651328 | bytes 11223697 | solution.py:88
  74.4 0.1 iota_compare_fusion.4
  74.5 0.1 broadcast_in_dim.43
  74.5 0.7 fusion.71
  75.2 0.6 fusion.72
  75.8 1.0 %fusion.73 = bf16[2,512,64]{1,2,0:T(8,128)(2,1)S(1)} fusion(bf16[2,512,64]{1,2,0:T(8,128)(2,1)S(1)} %get-tuple-element.130, s32[]{:T(128)} %get-tuple-element.129, f32[512,1536]{1,0:T(8,128)S(1)} %get-tuple-element.121, f32[512]{0:T(512)S(1)} %fusion.72, f32[512]{0:T(512)S(1)} %get-tuple-element.122, ...), kind=kOutput, calls=%fused_computation.9.clone.1 | convolution fusion | flops 103055360 | bytes 3608580 | tf_op jit(solution)/shard_map/while/body/eval_jaxpr/while/body/eval_jaxpr/dot_general | solution.py:47
  76.8 0.1 iota_compare_fusion.4
  76.9 0.1 broadcast_in_dim.43
  77.0 0.7 fusion.71
  77.7 0.6 fusion.72
  78.3 1.0 %fusion.73 = bf16[2,512,64]{1,2,0:T(8,128)(2,1)S(1)} fusion(bf16[2,512,64]{1,2,0:T(8,128)(2,1)S(1)} %get-tuple-element.130, s32[]{:T(128)} %get-tuple-element.129, f32[512,1536]{1,0:T(8,128)S(1)} %get-tuple-element.121, f32[512]{0:T(512)S(1)} %fusion.72, f32[512]{0:T(512)S(1)} %get-tuple-element.122, ...), kind=kOutput, calls=%fused_computation.9.clone.1 | convolution fusion | flops 103055360 | bytes 3608580 | tf_op jit(solution)/shard_map/while/body/eval_jaxpr/while/body/eval_jaxpr/dot_general | solution.py:47
  79.3 0.2 copy.30
  79.4 0.1 reshape.52
  79.6 10.5 %all_to_all.15 = bf16[16,32,128]{2,1,0:T(8,128)(2,1)S(1)} all-to-all(bf16[16,32,128]{2,1,0:T(8,128)(2,1)S(1)} %reshape.52), channel_id=1, replica_groups=mesh['groups'=2,'tok'=16] {'tok'}, dimensions={0} | all-to-all | bytes 262144 | tf_op jit(solution)/shard_map/all_to_all | solution.py:90
  90.1 0.1 copy.31
  90.1 4.6 %convolution_convert_fusion.1 = bf16[32,1536]{1,0:T(8,128)(2,1)} fusion(bf16[2048,1536]{1,0:T(8,128)(2,1)} %param.20, bf16[4,8,16,128]{3,2,1,0:T(8,128)(2,1)S(1)} %bitcast.112), kind=kOutput, calls=%fused_computation.18 | convolution fusion | flops 201375744 | bytes 6520832 | tf_op jit(solution)/shard_map/dot_general | solution.py:93
  (11 shorter events, 0.2 us)
Async XLA Ops:
  0.0 11.6 %copy-start = (f32[4096,32]{0,1:T(8,128)S(1)}, f32[4096,32]{0,1:T(8,128)}, u32[]{:S(2)}) copy-start(f32[4096,32]{0,1:T(8,128)} %param.18) | copy-start | bytes 1572868
  1.7 39.1 %all-to-all-start = ((bf16[16,32,128]{2,1,0:T(8,128)(2,1)}), bf16[16,32,128]{2,1,0:T(8,128)(2,1)S(1)}, u32[]{:S(2)}, u32[]{:S(2)}) async-start(bf16[16,32,128]{2,1,0:T(8,128)(2,1)} %bitcast.103), calls=%async_computation | async-start | bytes 262144 | tf_op jit(solution)/shard_map/all_to_all | solution.py:74
  40.8 28.6 %all-to-all-start.1 = ((bf16[16,32,256]{2,1,0:T(8,128)(2,1)}), bf16[16,32,256]{2,1,0:T(8,128)(2,1)S(1)}, u32[]{:S(2)}, u32[]{:S(2)}) async-start(bf16[16,32,256]{2,1,0:T(8,128)(2,1)} %bitcast.102), calls=%async_computation.1 | async-start | bytes 524288 | tf_op jit(solution)/shard_map/all_to_all | solution.py:78
  73.0 1.3 %copy-start.1 = (s32[16]{0:T(128)S(1)}, s32[16]{0:T(128)}, u32[]{:S(2)}) copy-start(s32[16]{0:T(128)} %param.17) | copy-start | bytes 196
where the time goes:
time: 95.2 us; the launch traced here: 94.7 us
  blocking collectives  32.8 us (34%)
  other arithmetic  24.6 us (26%)
  matrix products  17.5 us (18%)
  starting transfers between devices  13.4 us (14%)
  local copies, waits for them, and re-layouts  5.45 us (6%)
    all_gather x1, blocking collectives, per_device(): lax.all_gather(left_factor, 'tok', axis=0, tiled=True)  22.3 us
    another operation x9, other arithmetic, orthonormal(): lower_factor = jnp.linalg.cholesky(gram_matrix)  10.8 us
    all_to_all x1, blocking collectives, per_device(): lax.all_to_all(attended, 'tok', split_axis=0, concat_axis=0, tiled=True)  10.5 us
    another operation x6, other arithmetic, orthonormal(): jax.scipy.linalg.solve_triangular(lower_factor, block_cols.T, lower=True)  9.26 us
    all_to_all x1, starting transfers between devices, per_device(): lax.all_to_all(q_blocks, 'tok', split_axis=0, concat_axis=0, tiled=True)  7.39 us
    all_to_all x1, starting transfers between devices, per_device(): lax.all_to_all(w_blocks, 'tok', split_axis=0, concat_axis=0, tiled=True)  6.01 us
    dot_general x1, matrix products, per_device(): jnp.dot(row_block, w_out, preferred_element_type=jnp.float32)  4.56 us
    dot_general x2, matrix products, compress(): basis_cols = orthonormal(jnp.dot(delta_block, inner, precision=highest))  2.69 us
  transfers between devices with their start and end apart: 2, of which 0 were waited for; matrix products, arithmetic and copies ran while one was open for 33% of the time, Pallas kernels for 0%

commit v1 on v0

--- a/solution.py
+++ b/solution.py
@@ -87,7 +87,19 @@
     q_heads = q_here.reshape(query_count, per_dev, HD).transpose(1, 0, 2)
     attended = lax.map(lambda pieces: attend_head(pieces, live_keys), (q_heads, keys_values))
     attended = attended.transpose(1, 0, 2).reshape(shards, part_rows, per_dev * HD)
-    returned = lax.all_to_all(attended, "tok", split_axis=0, concat_axis=0, tiled=True)
+    ways, here = (lax.axis_size("tok"), lax.axis_index("tok"))
+    width_2 = attended.shape[0] // ways
+    lengths = list(attended.shape)
+    lengths[0] = width_2
+    height = lengths[0]
+    lengths[0] = height * ways
+    full = jnp.zeros(lengths, attended.dtype)
+    for mask in range(ways):
+        part = lax.dynamic_slice_in_dim(attended, (here ^ mask) * width_2, width_2, axis=0)
+        if mask:
+            part = lax.ppermute(part, "tok", [(d, d ^ mask) for d in range(ways)])
+        full = lax.dynamic_update_slice_in_dim(full, part, (here ^ mask) * height, axis=0)
+    returned = full
     returned = returned.reshape(head_groups, groups_q, part_rows, per_dev * HD)
     row_block = returned.transpose(1, 2, 0, 3).reshape(query_rows, head_count * HD)
     return jnp.dot(row_block, w_out, preferred_element_type=jnp.float32).astype(jnp.bfloat16)

time: 95.2 us -> 109 us (1.14)
  starting transfers between devices: 13.4 us -> 33.7 us
  blocking collectives: 32.8 us -> 22.3 us
  waiting for transfers between devices: 0.01 us -> 1.86 us
  local copies, waits for them, and re-layouts: 5.45 us -> 7.18 us
    ppermute x0 -> x15, starting transfers between devices: none -> 20.3 us  [per_device(): part = lax.ppermute(part, 'tok', [(d, d ^ mask) for d in range(ways)])]
    all_to_all x1 -> x0, blocking collectives: 10.5 us -> none  [per_device(): lax.all_to_all(attended, 'tok', split_axis=0, concat_axis=0, tiled=True)]
    ppermute x0 -> x15, waiting for transfers between devices: none -> 1.86 us  [per_device(): part = lax.ppermute(part, 'tok', [(d, d ^ mask) for d in range(ways)])]
    dynamic_update_slice x0 -> x16, local copies, waits for them, and re-layouts: none -> 1.45 us  [per_device(): lax.dynamic_update_slice_in_dim(full, part, (here ^ mask) * height, axis=0)]
  transfers between devices with their start and end apart: 2 -> 17, of which waited for: 0 -> 2; matrix products, arithmetic and copies ran while one was open for 33% -> 29% of each run, Pallas kernels for 0% -> 0%
where the time goes in v1:
time: 109 us; the launch traced here: 108 us
  starting transfers between devices  33.7 us (31%)
  other arithmetic  24.6 us (23%)
  blocking collectives  22.3 us (20%)
  matrix products  17.5 us (16%)
  local copies, waits for them, and re-layouts  7.18 us (7%)
  waiting for transfers between devices  1.86 us (2%)
  between operations  1.25 us (1%)
    all_gather x1, blocking collectives, per_device(): lax.all_gather(left_factor, 'tok', axis=0, tiled=True)  22.3 us
    ppermute x15, starting transfers between devices, per_device(): part = lax.ppermute(part, 'tok', [(d, d ^ mask) for d in range(ways)])  20.3 us
    another operation x9, other arithmetic, orthonormal(): lower_factor = jnp.linalg.cholesky(gram_matrix)  10.8 us
    another operation x6, other arithmetic, orthonormal(): jax.scipy.linalg.solve_triangular(lower_factor, block_cols.T, lower=True)  9.26 us
    all_to_all x1, starting transfers between devices, per_device(): lax.all_to_all(q_blocks, 'tok', split_axis=0, concat_axis=0, tiled=True)  7.39 us
    all_to_all x1, starting transfers between devices, per_device(): lax.all_to_all(w_blocks, 'tok', split_axis=0, concat_axis=0, tiled=True)  6.01 us
    dot_general x1, matrix products, per_device(): jnp.dot(row_block, w_out, preferred_element_type=jnp.float32)  4.56 us
    dot_general x2, matrix products, compress(): basis_cols = orthonormal(jnp.dot(delta_block, inner, precision=highest))  2.69 us
  transfers between devices with their start and end apart: 17, of which 2 were waited for; matrix products, arithmetic and copies ran while one was open for 29% of the time, Pallas kernels for 0%

profile of v1, /device:TPU:0, one launch (start us, length us, event | category | flops | bytes accessed | tf_op | source)
XLA Modules:
  0.0 108.5 jit_solution(15240968153499442122)
XLA Ops:
  0.0 1.0 copy.71
  1.0 0.7 copy.81
  1.7 7.4 %all-to-all-start = ((bf16[16,32,128]{2,1,0:T(8,128)(2,1)}), bf16[16,32,128]{2,1,0:T(8,128)(2,1)S(1)}, u32[]{:S(2)}, u32[]{:S(2)}) async-start(bf16[16,32,128]{2,1,0:T(8,128)(2,1)} %bitcast.118), calls=%async_computation | async-start | bytes 262144 | tf_op jit(solution)/shard_map/all_to_all | solution.py:74
  9.7 1.9 %bitcast_subtract_fusion = f32[96,4096]{1,0:T(8,128)S(1)} fusion(bf16[96,4096]{1,0:T(8,128)(2,1)} %param.14, bf16[2,96,4096]{2,1,0:T(8,128)(2,1)} %param.15, pred[]{:T(512)} %bitcast.3), kind=kLoop, calls=%fused_computation.21 | loop fusion | flops 1966080 | bytes 3932161 | tf_op jit(solution)/shard_map/sub | solution.py:68
  11.6 1.3 %fusion.37 = f32[96,32]{0,1:T(8,128)S(1)} fusion(f32[96,4096]{1,0:T(8,128)S(1)} %bitcast_subtract_fusion, f32[4096,32]{0,1:T(8,128)S(1)} %copy-done), kind=kOutput, calls=%fused_computation.77 | convolution fusion | flops 150994944 | bytes 2109440 | tf_op jit(solution)/shard_map/dot_general | solution.py:19
  13.0 0.1 fusion.38
  13.2 2.9 %cholesky.59 = f32[32,32]{1,0:T(8,128)S(1)} custom-call(f32[32,32]{1,0:T(8,128)S(1)} %fusion.31), custom_call_target="Cholesky" | custom-call | tf_op jit(solution)/shard_map/jit(cholesky)/cholesky | solution.py:14
  16.2 0.6 compare_reduce_fusion.2
  16.8 0.7 fusion.17
  17.5 2.4 %custom-call.7 = f32[1,32,32]{1,2,0:T(8,128)S(1)} custom-call(f32[1,32,32]{2,1,0:T(8,128)S(1)} %fusion.17), custom_call_target="InvertDiagBlocksLowerTriangular" | custom-call | tf_op jit(solution)/shard_map/jit(_solve_triangular)/triangular_solve | solution.py:15
  19.9 0.2 fusion.28
  20.1 1.0 fusion.39
  21.2 1.3 %fusion.40 = f32[96,32]{0,1:T(8,128)S(1)} fusion(f32[96,4096]{1,0:T(8,128)S(1)} %bitcast_subtract_fusion, f32[4096,32]{0,1:T(8,128)S(1)} %fusion.39), kind=kOutput, calls=%fused_computation.80 | convolution fusion | flops 150994944 | bytes 2109440 | tf_op jit(solution)/shard_map/dot_general | solution.py:22
  22.5 0.1 fusion.41
  22.7 2.9 %cholesky.70 = f32[32,32]{1,0:T(8,128)S(1)} custom-call(f32[32,32]{1,0:T(8,128)S(1)} %fusion.27), custom_call_target="Cholesky" | custom-call | tf_op jit(solution)/shard_map/jit(cholesky)/cholesky | solution.py:14
  25.7 0.6 compare_reduce_fusion.1
  26.3 0.7 fusion.18
  27.0 2.4 %custom-call.8 = f32[1,32,32]{1,2,0:T(8,128)S(1)} custom-call(f32[1,32,32]{2,1,0:T(8,128)S(1)} %fusion.18), custom_call_target="InvertDiagBlocksLowerTriangular" | custom-call | tf_op jit(solution)/shard_map/jit(_solve_triangular)/triangular_solve | solution.py:15
  29.4 0.2 fusion.24
  29.7 1.0 fusion.42
  30.7 1.3 %fusion.43 = f32[96,32]{0,1:T(8,128)S(1)} fusion(f32[96,4096]{1,0:T(8,128)S(1)} %bitcast_subtract_fusion, f32[4096,32]{0,1:T(8,128)S(1)} %fusion.42), kind=kOutput, calls=%fused_computation.83 | convolution fusion | flops 150994944 | bytes 2109440 | tf_op jit(solution)/shard_map/dot_general | solution.py:22
  32.0 0.1 fusion.44
  32.3 2.9 %cholesky.81 = f32[32,32]{1,0:T(8,128)S(1)} custom-call(f32[32,32]{1,0:T(8,128)S(1)} %fusion.23), custom_call_target="Cholesky" | custom-call | tf_op jit(solution)/shard_map/jit(cholesky)/cholesky | solution.py:14
  35.2 0.6 compare_reduce_fusion
  35.9 0.7 fusion.19
  36.5 2.4 %custom-call.9 = f32[1,32,32]{1,2,0:T(8,128)S(1)} custom-call(f32[1,32,32]{2,1,0:T(8,128)S(1)} %fusion.19), custom_call_target="InvertDiagBlocksLowerTriangular" | custom-call | tf_op jit(solution)/shard_map/jit(_solve_triangular)/triangular_solve | solution.py:15
  39.0 0.2 fusion.20
  39.2 0.9 convolution_convert_fusion
  40.1 0.7 copy.80
  40.8 6.0 %all-to-all-start.1 = ((bf16[16,32,256]{2,1,0:T(8,128)(2,1)}), bf16[16,32,256]{2,1,0:T(8,128)(2,1)S(1)}, u32[]{:S(2)}, u32[]{:S(2)}) async-start(bf16[16,32,256]{2,1,0:T(8,128)(2,1)} %bitcast.117), calls=%async_computation.1 | async-start | bytes 524288 | tf_op jit(solution)/shard_map/all_to_all | solution.py:78
  46.9 22.3 %all-gather = bf16[16,96,32]{1,2,0:T(8,128)(2,1)S(1)} all-gather(bf16[1,96,32]{1,2,0:T(8,128)(2,1)S(1)} %convert_bitcast_fusion), channel_id=1, replica_groups=mesh['groups'=2,'tok'=16] {'tok'}, dimensions={0}, use_global_device_ids=true | all-gather | bytes 104448 | tf_op jit(solution)/shard_map/all_gather | solution.py:75
  69.3 0.1 reshape.114
  69.5 1.6 %fusion.14 = f32[16,96,256]{2,1,0:T(8,128)} fusion(bf16[16,96,32]{1,2,0:T(8,128)(2,1)S(1)} %all-gather, bf16[16,32,256]{2,1,0:T(8,128)(2,1)S(1)} %all-to-all-done.1), kind=kOutput, calls=%fused_computation.23 | convolution fusion | flops 25952256 | bytes 1933312 | tf_op jit(solution)/shard_map/str,src->stc/dot_general | solution.py:79
  71.0 2.1 %reshape.135 = f32[1536,2,128]{2,1,0:T(2,128)S(1)} reshape(f32[16,96,256]{2,1,0:T(8,128)} %fusion.14) | data formatting | bytes 3145728 | tf_op jit(solution)/shard_map/convert_element_type | solution.py:83
  73.1 1.3 %fusion.13 = bf16[2,1536,128]{2,1,0:T(8,128)(2,1)S(1)} fusion(f32[1536,2,128]{2,1,0:T(2,128)S(1)} %reshape.135, bf16[2,1536,128]{2,1,0:T(8,128)(2,1)} %param.19), kind=kLoop, calls=%fused_computation.20 | loop fusion | flops 1179648 | bytes 3145728 | tf_op jit(solution)/shard_map/convert_element_type | solution.py:83
  74.4 4.9 %while.11 = (s32[]{:T(128)}, bf16[2,512,64]{1,2,0:T(8,128)(2,1)S(1)}, bf16[2,512,64]{2,1,0:T(8,128)(2,1)S(1)}, bf16[2,1536,128]{2,1,0:T(8,128)(2,1)S(1)}, s32[16]{0:T(128)S(1)}, /*index=5*/s32[]{:T(128)}) while((s32[]{:T(128)}, bf16[2,512,64]{1,2,0:T(8,128)(2,1)S(1)}, bf16[2,512,64]{2,1,0:T(8,128)(2,1)S(1)}, ...), condition=%wide.region_5.8_spmd.clone, body=%wide.region_2.7_spmd.clone.sunk | while | flops 207651328 | bytes 11223697 | solution.py:88
  74.6 0.7 fusion.71
  75.3 0.6 fusion.72
  75.9 1.0 fusion.73
  77.1 0.7 fusion.71
  77.8 0.6 fusion.72
  78.4 1.0 fusion.73
  79.3 0.2 copy.53
  79.5 0.1 reshape.117
  79.7 0.1 constant_dynamic-slice_fusion
  79.8 0.4 collective-permute-start
  80.2 0.2 collective-permute-start.1
  80.4 1.3 %collective-permute-start.2 = (bf16[1,32,128]{2,1,0:T(8,128)(2,1)S(1)}, bf16[1,32,128]{2,1,0:T(8,128)(2,1)S(1)}, u32[]{:S(2)}, u32[]{:S(2)}) collective-permute-start(bf16[1,32,128]{2,1,0:T(8,128)(2,1)S(1)} %get-tuple-element.105), channel_id=1, source_target_pairs={{0,3},{1,2},{2,1},{3,0},{4,7},{5,6},{6,5},{7,4},{8,11},{9,10},{10,... | collective-permute-start | bytes 24584 | tf_op jit(solution)/shard_map/ppermute | solution.py:100
  81.7 2.0 %collective-permute-start.4 = (bf16[1,32,128]{2,1,0:T(8,128)(2,1)S(1)}, bf16[1,32,128]{2,1,0:T(8,128)(2,1)S(1)}, u32[]{:S(2)}, u32[]{:S(2)}) collective-permute-start(bf16[1,32,128]{2,1,0:T(8,128)(2,1)S(1)} %get-tuple-element.103), channel_id=1, source_target_pairs={{0,5},{1,4},{2,7},{3,6},{4,1},{5,0},{6,3},{7,2},{8,13},{9,12},{10,... | collective-permute-start | bytes 24584 | tf_op jit(solution)/shard_map/ppermute | solution.py:100
  83.7 0.2 collective-permute-done.1
  83.8 2.3 %collective-permute-start.6 = (bf16[1,32,128]{2,1,0:T(8,128)(2,1)S(1)}, bf16[1,32,128]{2,1,0:T(8,128)(2,1)S(1)}, u32[]{:S(2)}, u32[]{:S(2)}) collective-permute-start(bf16[1,32,128]{2,1,0:T(8,128)(2,1)S(1)} %get-tuple-element.101), channel_id=1, source_target_pairs={{0,7},{1,6},{2,5},{3,4},{4,3},{5,2},{6,1},{7,0},{8,15},{9,14},{10,... | collective-permute-start | bytes 24584 | tf_op jit(solution)/shard_map/ppermute | solution.py:100
  86.1 2.9 %collective-permute-start.8 = (bf16[1,32,128]{2,1,0:T(8,128)(2,1)S(1)}, bf16[1,32,128]{2,1,0:T(8,128)(2,1)S(1)}, u32[]{:S(2)}, u32[]{:S(2)}) collective-permute-start(bf16[1,32,128]{2,1,0:T(8,128)(2,1)S(1)} %get-tuple-element.99), channel_id=1, source_target_pairs={{0,9},{1,8},{2,11},{3,10},{4,13},{5,12},{6,15},{7,14},{8,1},{9,0},... | collective-permute-start | bytes 24584 | tf_op jit(solution)/shard_map/ppermute | solution.py:100
  89.1 3.2 %collective-permute-start.10 = (bf16[1,32,128]{2,1,0:T(8,128)(2,1)S(1)}, bf16[1,32,128]{2,1,0:T(8,128)(2,1)S(1)}, u32[]{:S(2)}, u32[]{:S(2)}) collective-permute-start(bf16[1,32,128]{2,1,0:T(8,128)(2,1)S(1)} %get-tuple-element.97), channel_id=1, source_target_pairs={{0,11},{1,10},{2,9},{3,8},{4,15},{5,14},{6,13},{7,12},{8,3},{9,2},... | collective-permute-start | bytes 24584 | tf_op jit(solution)/shard_map/ppermute | solution.py:100
  92.3 3.8 %collective-permute-start.12 = (bf16[1,32,128]{2,1,0:T(8,128)(2,1)S(1)}, bf16[1,32,128]{2,1,0:T(8,128)(2,1)S(1)}, u32[]{:S(2)}, u32[]{:S(2)}) collective-permute-start(bf16[1,32,128]{2,1,0:T(8,128)(2,1)S(1)} %get-tuple-element.95), channel_id=1, source_target_pairs={{0,13},{1,12},{2,15},{3,14},{4,9},{5,8},{6,11},{7,10},{8,5},{9,4},... | collective-permute-start | bytes 24584 | tf_op jit(solution)/shard_map/ppermute | solution.py:100
  96.1 0.2 collective-permute-start.13
  96.3 4.0 %collective-permute-start.14 = (bf16[1,32,128]{2,1,0:T(8,128)(2,1)S(1)}, bf16[1,32,128]{2,1,0:T(8,128)(2,1)S(1)}, u32[]{:S(2)}, u32[]{:S(2)}) collective-permute-start(bf16[1,32,128]{2,1,0:T(8,128)(2,1)S(1)} %get-tuple-element.93), channel_id=1, source_target_pairs={{0,15},{1,14},{2,13},{3,12},{4,11},{5,10},{6,9},{7,8},{8,7},{9,6},... | collective-permute-start | bytes 24584 | tf_op jit(solution)/shard_map/ppermute | solution.py:100
  100.4 0.1 dynamic_update_slice.71
  100.8 1.7 %collective-permute-done.13 = bf16[1,32,128]{2,1,0:T(8,128)(2,1)S(1)} collective-permute-done((bf16[1,32,128]{2,1,0:T(8,128)(2,1)S(1)}, bf16[1,32,128]{2,1,0:T(8,128)(2,1)S(1)}, u32[]{:S(2)}, u32[]{:S(2)}) %collective-permute-start.13) | collective-permute-done | bytes 8224 | tf_op jit(solution)/shard_map/ppermute | solution.py:100
  102.5 0.1 dynamic_update_slice.72
  102.7 0.1 dynamic_update_slice.74
  102.8 0.1 dynamic_update_slice.75
  103.2 0.1 dynamic_update_slice.80
  103.3 0.1 dynamic_update_slice.81
  103.9 4.6 %convolution_convert_fusion.1 = bf16[32,1536]{1,0:T(8,128)(2,1)} fusion(bf16[2048,1536]{1,0:T(8,128)(2,1)} %param.20, bf16[4,8,16,128]{3,2,1,0:T(8,128)(2,1)S(1)} %bitcast.127), kind=kOutput, calls=%fused_computation.18 | convolution fusion | flops 201375744 | bytes 6520832 | tf_op jit(solution)/shard_map/dot_general | solution.py:105
  (69 shorter events, 2.1 us)
Async XLA Ops:
  0.0 11.6 %copy-start = (f32[4096,32]{0,1:T(8,128)S(1)}, f32[4096,32]{0,1:T(8,128)}, u32[]{:S(2)}) copy-start(f32[4096,32]{0,1:T(8,128)} %param.18) | copy-start | bytes 1572868
  1.7 39.1 %all-to-all-start = ((bf16[16,32,128]{2,1,0:T(8,128)(2,1)}), bf16[16,32,128]{2,1,0:T(8,128)(2,1)S(1)}, u32[]{:S(2)}, u32[]{:S(2)}) async-start(bf16[16,32,128]{2,1,0:T(8,128)(2,1)} %bitcast.118), calls=%async_computation | async-start | bytes 262144 | tf_op jit(solution)/shard_map/all_to_all | solution.py:74
  40.8 28.7 %all-to-all-start.1 = ((bf16[16,32,256]{2,1,0:T(8,128)(2,1)}), bf16[16,32,256]{2,1,0:T(8,128)(2,1)S(1)}, u32[]{:S(2)}, u32[]{:S(2)}) async-start(bf16[16,32,256]{2,1,0:T(8,128)(2,1)} %bitcast.117), calls=%async_computation.1 | async-start | bytes 524288 | tf_op jit(solution)/shard_map/all_to_all | solution.py:78
  73.1 1.3 %copy-start.1 = (s32[16]{0:T(128)S(1)}, s32[16]{0:T(128)}, u32[]{:S(2)}) copy-start(s32[16]{0:T(128)} %param.17) | copy-start | bytes 196
  79.8 3.9 %collective-permute-start = (bf16[1,32,128]{2,1,0:T(8,128)(2,1)S(1)}, bf16[1,32,128]{2,1,0:T(8,128)(2,1)S(1)}, u32[]{:S(2)}, u32[]{:S(2)}) collective-permute-start(bf16[1,32,128]{2,1,0:T(8,128)(2,1)S(1)} %get-tuple-element.107), channel_id=1, source_target_pairs={{0,1},{1,0},{2,3},{3,2},{4,5},{5,4},{6,7},{7,6},{8,9},{9,8},{10,11... | collective-permute-start | bytes 24584 | tf_op jit(solution)/shard_map/ppermute | solution.py:100
  80.2 3.7 %collective-permute-start.1 = (bf16[1,32,128]{2,1,0:T(8,128)(2,1)S(1)}, bf16[1,32,128]{2,1,0:T(8,128)(2,1)S(1)}, u32[]{:S(2)}, u32[]{:S(2)}) collective-permute-start(bf16[1,32,128]{2,1,0:T(8,128)(2,1)S(1)} %get-tuple-element.106), channel_id=1, source_target_pairs={{0,2},{1,3},{2,0},{3,1},{4,6},{5,7},{6,4},{7,5},{8,10},{9,11},{10,... | collective-permute-start | bytes 24584 | tf_op jit(solution)/shard_map/ppermute | solution.py:100
  80.4 5.7 %collective-permute-start.2 = (bf16[1,32,128]{2,1,0:T(8,128)(2,1)S(1)}, bf16[1,32,128]{2,1,0:T(8,128)(2,1)S(1)}, u32[]{:S(2)}, u32[]{:S(2)}) collective-permute-start(bf16[1,32,128]{2,1,0:T(8,128)(2,1)S(1)} %get-tuple-element.105), channel_id=1, source_target_pairs={{0,3},{1,2},{2,1},{3,0},{4,7},{5,6},{6,5},{7,4},{8,11},{9,10},{10,... | collective-permute-start | bytes 24584 | tf_op jit(solution)/shard_map/ppermute | solution.py:100
  81.7 4.4 %collective-permute-start.3 = (bf16[1,32,128]{2,1,0:T(8,128)(2,1)S(1)}, bf16[1,32,128]{2,1,0:T(8,128)(2,1)S(1)}, u32[]{:S(2)}, u32[]{:S(2)}) collective-permute-start(bf16[1,32,128]{2,1,0:T(8,128)(2,1)S(1)} %get-tuple-element.104), channel_id=1, source_target_pairs={{0,4},{1,5},{2,6},{3,7},{4,0},{5,1},{6,2},{7,3},{8,12},{9,13},{10,... | collective-permute-start | bytes 24584 | tf_op jit(solution)/shard_map/ppermute | solution.py:100
  81.7 7.3 %collective-permute-start.4 = (bf16[1,32,128]{2,1,0:T(8,128)(2,1)S(1)}, bf16[1,32,128]{2,1,0:T(8,128)(2,1)S(1)}, u32[]{:S(2)}, u32[]{:S(2)}) collective-permute-start(bf16[1,32,128]{2,1,0:T(8,128)(2,1)S(1)} %get-tuple-element.103), channel_id=1, source_target_pairs={{0,5},{1,4},{2,7},{3,6},{4,1},{5,0},{6,3},{7,2},{8,13},{9,12},{10,... | collective-permute-start | bytes 24584 | tf_op jit(solution)/shard_map/ppermute | solution.py:100
  83.7 5.4 %collective-permute-start.5 = (bf16[1,32,128]{2,1,0:T(8,128)(2,1)S(1)}, bf16[1,32,128]{2,1,0:T(8,128)(2,1)S(1)}, u32[]{:S(2)}, u32[]{:S(2)}) collective-permute-start(bf16[1,32,128]{2,1,0:T(8,128)(2,1)S(1)} %get-tuple-element.102), channel_id=1, source_target_pairs={{0,6},{1,7},{2,4},{3,5},{4,2},{5,3},{6,0},{7,1},{8,14},{9,15},{10,... | collective-permute-start | bytes 24584 | tf_op jit(solution)/shard_map/ppermute | solution.py:100
  83.8 8.5 %collective-permute-start.6 = (bf16[1,32,128]{2,1,0:T(8,128)(2,1)S(1)}, bf16[1,32,128]{2,1,0:T(8,128)(2,1)S(1)}, u32[]{:S(2)}, u32[]{:S(2)}) collective-permute-start(bf16[1,32,128]{2,1,0:T(8,128)(2,1)S(1)} %get-tuple-element.101), channel_id=1, source_target_pairs={{0,7},{1,6},{2,5},{3,4},{4,3},{5,2},{6,1},{7,0},{8,15},{9,14},{10,... | collective-permute-start | bytes 24584 | tf_op jit(solution)/shard_map/ppermute | solution.py:100
  86.1 6.2 %collective-permute-start.7 = (bf16[1,32,128]{2,1,0:T(8,128)(2,1)S(1)}, bf16[1,32,128]{2,1,0:T(8,128)(2,1)S(1)}, u32[]{:S(2)}, u32[]{:S(2)}) collective-permute-start(bf16[1,32,128]{2,1,0:T(8,128)(2,1)S(1)} %get-tuple-element.100), channel_id=1, source_target_pairs={{0,8},{1,9},{2,10},{3,11},{4,12},{5,13},{6,14},{7,15},{8,0},{9,1},... | collective-permute-start | bytes 24584 | tf_op jit(solution)/shard_map/ppermute | solution.py:100
  86.1 10.0 %collective-permute-start.8 = (bf16[1,32,128]{2,1,0:T(8,128)(2,1)S(1)}, bf16[1,32,128]{2,1,0:T(8,128)(2,1)S(1)}, u32[]{:S(2)}, u32[]{:S(2)}) collective-permute-start(bf16[1,32,128]{2,1,0:T(8,128)(2,1)S(1)} %get-tuple-element.99), channel_id=1, source_target_pairs={{0,9},{1,8},{2,11},{3,10},{4,13},{5,12},{6,15},{7,14},{8,1},{9,0},... | collective-permute-start | bytes 24584 | tf_op jit(solution)/shard_map/ppermute | solution.py:100
  89.0 7.3 %collective-permute-start.9 = (bf16[1,32,128]{2,1,0:T(8,128)(2,1)S(1)}, bf16[1,32,128]{2,1,0:T(8,128)(2,1)S(1)}, u32[]{:S(2)}, u32[]{:S(2)}) collective-permute-start(bf16[1,32,128]{2,1,0:T(8,128)(2,1)S(1)} %get-tuple-element.98), channel_id=1, source_target_pairs={{0,10},{1,11},{2,8},{3,9},{4,14},{5,15},{6,12},{7,13},{8,2},{9,3},... | collective-permute-start | bytes 24584 | tf_op jit(solution)/shard_map/ppermute | solution.py:100
  89.1 11.6 %collective-permute-start.10 = (bf16[1,32,128]{2,1,0:T(8,128)(2,1)S(1)}, bf16[1,32,128]{2,1,0:T(8,128)(2,1)S(1)}, u32[]{:S(2)}, u32[]{:S(2)}) collective-permute-start(bf16[1,32,128]{2,1,0:T(8,128)(2,1)S(1)} %get-tuple-element.97), channel_id=1, source_target_pairs={{0,11},{1,10},{2,9},{3,8},{4,15},{5,14},{6,13},{7,12},{8,3},{9,2},... | collective-permute-start | bytes 24584 | tf_op jit(solution)/shard_map/ppermute | solution.py:100
  92.3 8.4 %collective-permute-start.11 = (bf16[1,32,128]{2,1,0:T(8,128)(2,1)S(1)}, bf16[1,32,128]{2,1,0:T(8,128)(2,1)S(1)}, u32[]{:S(2)}, u32[]{:S(2)}) collective-permute-start(bf16[1,32,128]{2,1,0:T(8,128)(2,1)S(1)} %get-tuple-element.96), channel_id=1, source_target_pairs={{0,12},{1,13},{2,14},{3,15},{4,8},{5,9},{6,10},{7,11},{8,4},{9,5},... | collective-permute-start | bytes 24584 | tf_op jit(solution)/shard_map/ppermute | solution.py:100
  92.3 8.4 %collective-permute-start.12 = (bf16[1,32,128]{2,1,0:T(8,128)(2,1)S(1)}, bf16[1,32,128]{2,1,0:T(8,128)(2,1)S(1)}, u32[]{:S(2)}, u32[]{:S(2)}) collective-permute-start(bf16[1,32,128]{2,1,0:T(8,128)(2,1)S(1)} %get-tuple-element.95), channel_id=1, source_target_pairs={{0,13},{1,12},{2,15},{3,14},{4,9},{5,8},{6,11},{7,10},{8,5},{9,4},... | collective-permute-start | bytes 24584 | tf_op jit(solution)/shard_map/ppermute | solution.py:100
  96.1 6.3 %collective-permute-start.13 = (bf16[1,32,128]{2,1,0:T(8,128)(2,1)S(1)}, bf16[1,32,128]{2,1,0:T(8,128)(2,1)S(1)}, u32[]{:S(2)}, u32[]{:S(2)}) collective-permute-start(bf16[1,32,128]{2,1,0:T(8,128)(2,1)S(1)} %get-tuple-element.94), channel_id=1, source_target_pairs={{0,14},{1,15},{2,12},{3,13},{4,10},{5,11},{6,8},{7,9},{8,6},{9,7},... | collective-permute-start | bytes 24584 | tf_op jit(solution)/shard_map/ppermute | solution.py:100
  96.3 6.2 %collective-permute-start.14 = (bf16[1,32,128]{2,1,0:T(8,128)(2,1)S(1)}, bf16[1,32,128]{2,1,0:T(8,128)(2,1)S(1)}, u32[]{:S(2)}, u32[]{:S(2)}) collective-permute-start(bf16[1,32,128]{2,1,0:T(8,128)(2,1)S(1)} %get-tuple-element.93), channel_id=1, source_target_pairs={{0,15},{1,14},{2,13},{3,12},{4,11},{5,10},{6,9},{7,8},{8,7},{9,6},... | collective-permute-start | bytes 24584 | tf_op jit(solution)/shard_map/ppermute | solution.py:100
